TPU v7x, 32 devices: a whole 2x2x4 slice. The times are simulated.
32 devices in a mesh: groups: 2 (over y), dp: 8 (over z, x), section: 2 (over core).
Axes of the slice: x: 2, y: 2, z: 4, core: 2. Of those that a mesh axis runs over, the one named last changes fastest.
Arguments:
- boundary: bfloat16 [2, 32, 64, 8192], P('section', ('groups', 'dp')), parts along dimension 1, may hold values from -6 to 6
- w_query: bfloat16 [2, 8192, 128], P('section', 'dp'), may hold values from -8 to 8
- w_key: bfloat16 [2, 8192, 128], P('section', 'dp'), may hold values from -1 to 1
- w_value: bfloat16 [2, 8192, 128], P('section', 'dp'), may hold values from -0.0625 to 0.0625
- w_out: bfloat16 [2, 128, 8192], P('section', None, 'dp'), may hold values from -0.5 to 0.5
- norm_gain: bfloat16 [2, 8192], P('section'), may hold values from 0.099609375 to 1.8984375
- proj_wide: bfloat16 [64, 8192], replicated, may hold values from -0.0625 to 0.0625
- proj_head: bfloat16 [2, 2, 64, 128], P('section'), may hold values from -0.5 to 0.5
- lengths: int32 [32], P(('groups', 'dp')), parts along dimension 0, may hold values from 1 to 64, 614 in all
- owners: int32 [32, 1], P(('groups', 'dp')), parts along dimension 0, may hold values from 0 to 7; in each aligned block of 16 rows (0 to 15, 16 to 31, ...) at most 4 rows name the same one
Outputs:
- store: bfloat16 [64, 2, 2, 64, 64], P(('groups', 'dp'), 'section'), parts along dimension 0
There are 2 independent parts, one for each index of `groups`. A program takes and returns all parts, laid end to end along the dimension named above; an argument that names none is the same for every part. Nothing has to cross between parts.
Inputs may be any that keep to these rules, and one draw needn't show every extreme that they name: `owners`: every owner is named by at most 4 examples, a bound that some block reaches. `lengths`: some sequence has exactly 64 tokens.
All inputs are finite; a program needn't handle non-finite values. No bound on the sum of `lengths` on one device may be relied on, other than what follows from the above.
Results may differ from a plain program's by a relative error of at most 0.013.
Values may be sent and summed in bfloat16 or wider, within the bound.
A program may use at most 128 MiB of HBM per device.

v0:
```python
import jax
import jax.numpy as jnp
from jax import lax
from jax.sharding import PartitionSpec as P

CAP = 4
EPSILON = 1e-05
MASKED = -1e30


def passed_along(array, axis, by):
    size = lax.axis_size(axis)
    pairs = [(i, i + by) for i in range(size) if 0 <= i + by < size]
    return lax.ppermute(array, axis, pairs)


def for_sending(array):

    def short(part):
        return part.astype(jnp.bfloat16) if part.dtype == jnp.float32 else part

    return jax.tree.map(short, array)


def section_forward(hidden, zero_probe, w_query, w_key, w_value, w_out, section_gain, seq_length):
    token_count = hidden.shape[0]
    head_size = w_query.shape[1]
    widened = hidden.astype(jnp.float32)
    inverse_rms = lax.rsqrt(jnp.mean(widened * widened, axis=-1, keepdims=True) + EPSILON)
    normed = (widened * inverse_rms * section_gain.astype(jnp.float32)).astype(jnp.bfloat16)
    queries = jnp.dot(normed, w_query, preferred_element_type=jnp.float32).astype(jnp.bfloat16)
    key_vecs = jnp.dot(normed, w_key, preferred_element_type=jnp.float32).astype(jnp.bfloat16)
    values = (
        jnp.dot(normed, w_value, preferred_element_type=jnp.float32).astype(jnp.bfloat16)
        + zero_probe
    )
    scores = lax.dot_general(
        queries, key_vecs, (((1,), (1,)), ((), ())), preferred_element_type=jnp.float32
    ) * head_size ** (-0.5)
    positions = jnp.arange(token_count)
    allowed = (positions[None, :] <= positions[:, None]) & (positions[None, :] < seq_length)
    scores = jnp.where(allowed, scores, MASKED)
    highest = jnp.max(scores, axis=-1, keepdims=True)
    expd = jnp.exp(scores - highest)
    probs = (expd / jnp.sum(expd, axis=-1, keepdims=True)).astype(jnp.bfloat16)
    mixed = jnp.dot(probs, values, preferred_element_type=jnp.float32).astype(jnp.bfloat16)
    result = (widened + jnp.dot(mixed, w_out, preferred_element_type=jnp.float32)).astype(
        jnp.bfloat16
    )
    return (result, (normed, mixed))


def module_blocks(normed, mixed, value_grad, cotangent, proj_wide, head_proj, valid):
    contract = (((1,), (1,)), ((), ()))
    across = (((0,), (0,)), ((), ()))
    valid_col = valid[:, None]
    wide_in = lax.dot_general(
        normed, proj_wide, contract, preferred_element_type=jnp.float32
    ).astype(jnp.bfloat16)
    head_in = lax.dot_general(
        mixed, head_proj[1], contract, preferred_element_type=jnp.float32
    ).astype(jnp.bfloat16)
    value_side = jnp.where(
        valid_col,
        lax.dot_general(value_grad, head_proj[0], contract, preferred_element_type=jnp.float32),
        0.0,
    ).astype(jnp.bfloat16)
    wide_out = jnp.where(
        valid_col,
        lax.dot_general(cotangent, proj_wide, contract, preferred_element_type=jnp.float32),
        0.0,
    ).astype(jnp.bfloat16)
    block_value = lax.dot_general(value_side, wide_in, across, preferred_element_type=jnp.float32)
    block_output = lax.dot_general(wide_out, head_in, across, preferred_element_type=jnp.float32)
    return jnp.stack([block_value, block_output]).astype(jnp.bfloat16)


def shards(
    boundary, w_query, w_key, w_value, w_out, norm_gain, proj_wide, proj_head, lengths, owners
):
    my_section = lax.axis_index("section")
    section_count = lax.axis_size("section")
    my_owner = lax.axis_index("dp")
    micro_count = boundary.shape[1]
    token_count = boundary.shape[2]
    model_width = boundary.shape[3]
    proj_rank = proj_wide.shape[0]
    query_w, key_w, value_w, out_w = (
        lax.all_gather(w_query[0], "dp", axis=0, tiled=True),
        lax.all_gather(w_key[0], "dp", axis=0, tiled=True),
        lax.all_gather(w_value[0], "dp", axis=0, tiled=True),
        lax.all_gather(w_out[0], "dp", axis=1, tiled=True),
    )
    all_owner = lax.all_gather(owners[:, 0], "dp", axis=0, tiled=True)
    ordinal = jnp.arange(all_owner.shape[0])
    earlier = (all_owner[None, :] == all_owner[:, None]) & (ordinal[None, :] < ordinal[:, None])
    all_slot = jnp.sum(earlier.astype(jnp.int32), axis=1)
    slot_ids = jnp.arange(CAP)[:, None]
    section_gain = norm_gain[0]
    head_proj = proj_head[0]
    boundary_slab = boundary[0]
    positions = jnp.arange(token_count)
    zero_probe = jnp.zeros((token_count, query_w.shape[1]), jnp.bfloat16)
    tick_count = micro_count + section_count - 1

    def make_layer(seq_length):

        def layer(hidden, probe_in):
            return section_forward(
                hidden, probe_in, query_w, key_w, value_w, out_w, section_gain, seq_length
            )

        return layer

    saved = jnp.zeros_like(boundary_slab)
    incoming = jnp.zeros((token_count, model_width), jnp.bfloat16)
    for moment in range(tick_count):
        micro_index = moment - my_section
        is_live = (micro_index >= 0) & (micro_index < micro_count)
        chosen_micro = jnp.clip(micro_index, 0, micro_count - 1)
        own_slab = lax.dynamic_index_in_dim(boundary_slab, chosen_micro, 0, keepdims=False)
        hidden = jnp.where(my_section == 0, own_slab, incoming)
        current = lax.dynamic_index_in_dim(saved, chosen_micro, 0, keepdims=False)
        saved = lax.dynamic_update_index_in_dim(
            saved, jnp.where(is_live, hidden, current), chosen_micro, 0
        )
        if moment + 1 < tick_count:
            seq_length = lax.dynamic_index_in_dim(lengths, chosen_micro, 0, keepdims=False)
            result, extra = make_layer(seq_length)(hidden, zero_probe)
            incoming = passed_along(result, "section", 1)
    blocks = jnp.zeros((micro_count, 2, proj_rank, proj_rank), jnp.bfloat16)
    incoming = jnp.zeros((token_count, model_width), jnp.bfloat16)
    for moment in range(tick_count):
        micro_index = moment - (section_count - 1 - my_section)
        is_live = (micro_index >= 0) & (micro_index < micro_count)
        chosen_micro = jnp.clip(micro_index, 0, micro_count - 1)
        seq_length = lax.dynamic_index_in_dim(lengths, chosen_micro, 0, keepdims=False)
        valid = positions < seq_length
        own_slab = lax.dynamic_index_in_dim(boundary_slab, chosen_micro, 0, keepdims=False)
        masked_own = jnp.where(valid[:, None], own_slab, jnp.zeros_like(own_slab))
        cotangent = jnp.where(my_section == section_count - 1, masked_own, incoming)
        hidden = lax.dynamic_index_in_dim(saved, chosen_micro, 0, keepdims=False)
        result, pullback, extra = jax.vjp(make_layer(seq_length), hidden, zero_probe, has_aux=True)
        hidden_grad, value_grad = pullback(cotangent)
        new_blocks = module_blocks(
            extra[0], extra[1], value_grad, cotangent, proj_wide, head_proj, valid
        )
        if moment + 1 < tick_count:
            incoming = jax.tree.map(
                lambda part, own: part.astype(own.dtype),
                passed_along(for_sending(hidden_grad), "section", -1),
                hidden_grad,
            )
        current = lax.dynamic_index_in_dim(blocks, chosen_micro, 0, keepdims=False)
        blocks = lax.dynamic_update_index_in_dim(
            blocks, jnp.where(is_live, new_blocks, current), chosen_micro, 0
        )
    piece = lax.all_gather(blocks, "dp", axis=0, tiled=True)
    piece_rows = piece.shape[0]
    picked = ((all_owner[None, :] == my_owner) & (all_slot[None, :] == slot_ids)).astype(
        jnp.bfloat16
    )
    running = jnp.dot(picked, piece.reshape(piece_rows, -1), preferred_element_type=jnp.float32)
    return running.astype(jnp.bfloat16).reshape(CAP, 1, 2, proj_rank, proj_rank)


def solution(mesh):
    return jax.shard_map(
        shards,
        mesh=mesh,
        in_specs=(
            P("section", ("groups", "dp"), None, None),
            P("section", "dp", None),
            P("section", "dp", None),
            P("section", "dp", None),
            P("section", None, "dp"),
            P("section", None),
            P(),
            P("section", None, None, None),
            P(("groups", "dp")),
            P(("groups", "dp"), None),
        ),
        out_specs=P(("groups", "dp"), "section", None, None, None),
        check_vma=False,
    )
```

profile of v0, /device:TPU:0, one launch (start us, length us, event | category | flops | bytes accessed | tf_op | source)
XLA Modules:
  0.0 332.0 jit_solution(5913133050592107326)
XLA Ops:
  12.0 13.2 %all-reduce = s32[16]{0:T(128)S(1)} all-reduce(s32[16]{0:T(128)S(1)} %bitcast_dynamic-update-slice_fusion.3), channel_id=2, replica_groups=mesh['groups'=2,'dp'=8,'section'=2] {'dp'}, use_global_device_ids=true, to_apply=%add | all-reduce | flops 16 | bytes 128 | tf_op jit(solution)/shard_map/all_gather | solution.py:94
  27.5 1.6 fusion.18
  34.1 27.2 %all-gather.10.cloned.1.call-done = bf16[1,8192,128]{2,1,0:T(8,128)(2,1)} async-done(((bf16[1,1024,128]{2,1,0:T(8,128)(2,1)}), bf16[1,8192,128]{2,1,0:T(8,128)(2,1)}) %all-gather.10.cloned.1.call-update) | async-done | bytes 2097168 | tf_op jit(solution)/shard_map/all_gather | solution.py:89
  61.3 2.5 fusion.84
  63.8 47.3 %all-gather.12.cloned.1.call-done = bf16[1,8192,128]{2,1,0:T(8,128)(2,1)} async-done(((bf16[1,1024,128]{2,1,0:T(8,128)(2,1)}), bf16[1,8192,128]{2,1,0:T(8,128)(2,1)}) %all-gather.12.cloned.1.call-update) | async-done | bytes 2097168 | tf_op jit(solution)/shard_map/all_gather | solution.py:90
  111.1 2.6 fusion.285
  113.7 47.2 %all-gather.14.cloned.1.call-done = bf16[1,8192,128]{2,1,0:T(8,128)(2,1)} async-done(((bf16[1,1024,128]{2,1,0:T(8,128)(2,1)}), bf16[1,8192,128]{2,1,0:T(8,128)(2,1)}) %all-gather.14.cloned.1.call-update) | async-done | bytes 2097168 | tf_op jit(solution)/shard_map/all_gather | solution.py:91
  160.9 2.5 fusion.114
  163.3 47.2 %all-gather.16.cloned.1.call-done = bf16[1,128,8192]{2,1,0:T(8,128)(2,1)} async-done(((bf16[1,128,1024]{2,1,0:T(8,128)(2,1)}), bf16[1,128,8192]{2,1,0:T(8,128)(2,1)}) %all-gather.16.cloned.1.call-update) | async-done | bytes 2097168 | tf_op jit(solution)/shard_map/all_gather | solution.py:92
  210.5 3.6 %fusion = bf16[64,8192]{1,0:T(8,128)(2,1)} fusion(bf16[1,128,8192]{2,1,0:T(8,128)(2,1)} %all-gather.16.cloned.1.call-done, bf16[64,128]{1,0:T(8,128)(2,1)S(1)} %fusion.114, bf16[1,2,64,8192]{3,2,1,0:T(8,128)(2,1)} %param.10, s32[]{:T(128)S(6)} %min.20, pred[]{:T(512)S(6)} %eq.63, f32[64,64]{0,1:T(8,128)S(1)} %get-tuple-element.27, f32[64]{0:T(128)S(1)} %fusion.163, ...), kind=kOutput, calls=%fused_computation.2 | convolution fusion | flops 137383936 | bytes 4227589 | tf_op jit(solution)/shard_map/dot_general | solution.py:47
  216.8 2.5 fusion.129
  221.6 2.6 fusion.290
  224.2 2.4 fusion.117
  226.6 3.4 %fusion.1 = bf16[64,8192]{1,0:T(8,128)(2,1)} fusion(bf16[64,8192]{1,0:T(8,128)(2,1)} %copy-done.5, bf16[1,128,8192]{2,1,0:T(8,128)(2,1)} %all-gather.16.cloned.1.call-done, bf16[64,128]{1,0:T(8,128)(2,1)S(1)} %fusion.117, f32[64,64]{0,1:T(8,128)S(1)} %get-tuple-element.29, f32[64]{0:T(128)S(1)} %fusion.164, f32[64]{0:T(128)S(1)} %get-tuple-element.28), kind=kOutput, calls=%fused_computation.3 | convolution fusion | flops 136859648 | bytes 4227584 | tf_op jit(solution)/shard_map/dot_general | solution.py:47
  230.1 1.7 collective-permute-start.1
  231.8 1.8 bitcast_dynamic-update-slice_fusion.1
  238.8 1.9 fusion.141
  241.5 3.7 %convolution_convert_fusion.3 = bf16[64,8192]{1,0:T(8,128)(2,1)} fusion(bf16[1,8192,128]{2,1,0:T(8,128)(2,1)} %all-gather.10.cloned.1.call-done, bf16[64,128]{1,0:T(8,128)(2,1)S(1)} %fusion.105, f32[64,64]{0,1:T(8,128)S(1)} %get-tuple-element.14, pred[64,64]{0,1:T(32,128)(4,1)S(1)} %get-tuple-element.16, f32[64]{0:T(128)S(1)} %negate_divide_fusion.1, ...), kind=kOutput, calls=%fused_computation.7 | convolution fusion | flops 135823360 | bytes 3182912 | tf_op jit(solution)/shard_map/transpose(jvp())/dot_general | solution.py:31
  245.2 3.6 %convolution_convert_fusion.4 = bf16[64,8192]{1,0:T(8,128)(2,1)} fusion(bf16[1,8192,128]{2,1,0:T(8,128)(2,1)} %all-gather.12.cloned.1.call-done, bf16[64,128]{1,0:T(8,128)(2,1)S(1)} %fusion.90, f32[64,64]{0,1:T(8,128)S(1)} %get-tuple-element.14, pred[64,64]{0,1:T(32,128)(4,1)S(1)} %get-tuple-element.16, f32[64]{0:T(128)S(1)} %negate_divide_fusion.1, ...), kind=kOutput, calls=%fused_computation.8 | convolution fusion | flops 135823360 | bytes 3182912 | tf_op jit(solution)/shard_map/transpose(jvp())/dot_general | solution.py:32
  248.8 3.4 %fusion.24 = (f32[64]{0:T(128)S(1)}, f32[64]{0:T(128)S(1)}, f32[64,8192]{1,0:T(8,128)S(1)}) fusion(bf16[2,64,8192]{2,1,0:T(8,128)(2,1)S(1)} %bitcast_dynamic-update-slice_fusion, s32[]{:T(128)S(6)} %min.19, s32[]{:T(128)S(6)} %min.23, f32[8192]{0:T(1024)S(1)} %bitcast.284, bf16[64,8192]{1,0:T(8,128)(2,1)} %convolution_convert_fusion.3, ...), kind=kOutput, calls=%fused_computation.49 | convolution fusion | flops 139984768 | bytes 8438280 | tf_op jit(solution)/shard_map/transpose(jvp())/dot_general | solution.py:34
  252.2 1.8 fusion.16
  259.1 2.8 fusion.153
  261.8 1.8 fusion.143
  263.6 2.8 fusion.132
  266.9 3.6 %convolution_convert_fusion = bf16[64,8192]{1,0:T(8,128)(2,1)} fusion(bf16[1,8192,128]{2,1,0:T(8,128)(2,1)} %all-gather.10.cloned.1.call-done, bf16[64,128]{1,0:T(8,128)(2,1)S(1)} %fusion.108, f32[64,64]{0,1:T(8,128)S(1)} %get-tuple-element.10, pred[64,64]{0,1:T(32,128)(4,1)S(1)} %get-tuple-element.12, f32[64]{0:T(128)S(1)} %negate_divide_fusion, ...), kind=kOutput, calls=%fused_computation.4 | convolution fusion | flops 135823360 | bytes 3182912 | tf_op jit(solution)/shard_map/transpose(jvp())/dot_general | solution.py:31
  270.5 3.6 %convolution_convert_fusion.1 = bf16[64,8192]{1,0:T(8,128)(2,1)} fusion(bf16[1,8192,128]{2,1,0:T(8,128)(2,1)} %all-gather.12.cloned.1.call-done, bf16[64,128]{1,0:T(8,128)(2,1)S(1)} %fusion.93, f32[64,64]{0,1:T(8,128)S(1)} %get-tuple-element.10, pred[64,64]{0,1:T(32,128)(4,1)S(1)} %get-tuple-element.12, f32[64]{0:T(128)S(1)} %negate_divide_fusion, ...), kind=kOutput, calls=%fused_computation.5 | convolution fusion | flops 135823360 | bytes 3182912 | tf_op jit(solution)/shard_map/transpose(jvp())/dot_general | solution.py:32
  274.1 3.3 fusion.28
  281.7 2.2 fusion.297
  284.0 2.1 fusion.126
  286.4 3.1 fusion.135
  290.4 2.2 fusion.145
  292.7 31.4 %all_gather.23 = bf16[16,2,64,64]{3,2,1,0:T(8,128)(2,1)S(1)} all-gather(bf16[2,2,64,64]{3,2,1,0:T(8,128)(2,1)S(1)} %fusion.157), channel_id=1, replica_groups=mesh['groups'=2,'dp'=8,'section'=2] {'dp'}, dimensions={0}, use_global_device_ids=true | all-gather | bytes 294912 | tf_op jit(solution)/shard_map/all_gather | solution.py:158
  (115 shorter events, 35.4 us)
Async XLA Ops:
  6.5 232.2 %copy-start = (bf16[64,8192]{1,0:T(8,128)(2,1)S(1)}, bf16[64,8192]{1,0:T(8,128)(2,1)}, u32[]{:S(2)}) copy-start(bf16[64,8192]{1,0:T(8,128)(2,1)} %param.16) | copy-start | bytes 3145732
  6.5 54.8 %all-gather.10.cloned.1.call-start = ((), (), s32[]{:S(2)}) async-start(), calls=%async_computation | async-start | bytes 2359296 | tf_op jit(solution)/shard_map/all_gather | solution.py:89
  7.3 103.8 %all-gather.12.cloned.1.call-start = ((), (), s32[]{:S(2)}) async-start(), calls=%async_computation.1 | async-start | bytes 2359296 | tf_op jit(solution)/shard_map/all_gather | solution.py:90
  8.0 152.9 %all-gather.14.cloned.1.call-start = ((), (), s32[]{:S(2)}) async-start(), calls=%async_computation.2 | async-start | bytes 2359296 | tf_op jit(solution)/shard_map/all_gather | solution.py:91
  8.7 201.8 %all-gather.16.cloned.1.call-start = ((), (), s32[]{:S(2)}) async-start(), calls=%async_computation.3 | async-start | bytes 2359296 | tf_op jit(solution)/shard_map/all_gather | solution.py:92
  214.1 2.6 copy-start.1
  214.1 5.1 %collective-permute-start = (bf16[64,8192]{1,0:T(8,128)(2,1)}, bf16[64,8192]{1,0:T(8,128)(2,1)S(1)}, u32[]{:S(2)}, u32[]{:S(2)}) collective-permute-start(bf16[64,8192]{1,0:T(8,128)(2,1)} %fusion), channel_id=1, source_target_pairs={{0,1},{2,3},{4,5},{6,7},{8,9},{10,11},{12,13},{14,15},{16,17},{18,... | collective-permute-start | bytes 3145736 | tf_op jit(solution)/shard_map/ppermute | solution.py:14
  219.2 1.9 copy-start.10
  219.7 1.0 copy-start.5
  230.1 3.9 %copy-start.2 = (bf16[1,2,64,8192]{3,2,1,0:T(8,128)(2,1)S(1)}, bf16[1,2,64,8192]{3,2,1,0:T(8,128)(2,1)}, u32[]{:S(2)}) copy-start(bf16[1,2,64,8192]{3,2,1,0:T(8,128)(2,1)} %param.10) | copy-start | bytes 6291460
  230.1 3.9 %collective-permute-start.1 = (bf16[64,8192]{1,0:T(8,128)(2,1)}, bf16[64,8192]{1,0:T(8,128)(2,1)S(1)}, u32[]{:S(2)}, u32[]{:S(2)}) collective-permute-start(bf16[64,8192]{1,0:T(8,128)(2,1)} %fusion.1), channel_id=1, source_target_pairs={{0,1},{2,3},{4,5},{6,7},{8,9},{10,11},{12,13},{14,15},{16,17},{18,... | collective-permute-start | bytes 3145736 | tf_op jit(solution)/shard_map/ppermute | solution.py:14
  233.7 1.6 copy-start.11
  234.5 1.7 copy-start.8
  236.2 1.6 copy-start.6
  236.7 1.6 copy-start.14
  248.8 3.4 %copy-start.3 = (bf16[1,2,64,8192]{3,2,1,0:T(8,128)(2,1)S(1)}, bf16[1,2,64,8192]{3,2,1,0:T(8,128)(2,1)}, u32[]{:S(2)}) copy-start(bf16[1,2,64,8192]{3,2,1,0:T(8,128)(2,1)} %param.10) | copy-start | bytes 6291460
  252.2 3.3 copy-start.12
  254.0 2.0 copy-start.9
  254.0 5.0 %collective-permute-start.2 = (bf16[64,8192]{1,0:T(8,128)(2,1)}, bf16[64,8192]{1,0:T(8,128)(2,1)}, u32[]{:S(2)}, u32[]{:S(2)}) collective-permute-start(bf16[64,8192]{1,0:T(8,128)(2,1)} %fusion.16), channel_id=1, source_target_pairs={{1,0},{3,2},{5,4},{7,6},{9,8},{11,10},{13,12},{15,14},{17,16},{19,... | collective-permute-start | bytes 3145736 | tf_op jit(solution)/shard_map/ppermute | solution.py:14
  256.1 1.6 copy-start.7
  274.1 3.3 %copy-start.4 = (bf16[64,8192]{1,0:T(8,128)(2,1)S(1)}, bf16[64,8192]{1,0:T(8,128)(2,1)}, u32[]{:S(2)}) copy-start(bf16[64,8192]{1,0:T(8,128)(2,1)} %fusion.153) | copy-start | bytes 3145732
  277.4 3.1 copy-start.13
  279.0 7.4 %collective-permute-start.3 = (bf16[64,8192]{1,0:T(8,128)(2,1)}, bf16[64,8192]{1,0:T(8,128)(2,1)}, u32[]{:S(2)}, u32[]{:S(2)}) collective-permute-start(bf16[64,8192]{1,0:T(8,128)(2,1)} %fusion.17), channel_id=1, source_target_pairs={{1,0},{3,2},{5,4},{7,6},{9,8},{11,10},{13,12},{15,14},{17,16},{19,... | collective-permute-start | bytes 3145736 | tf_op jit(solution)/shard_map/ppermute | solution.py:14
Sparse Core Ops, SparseCore 0:
  9.5 51.8 all-gather.9
  63.4 47.6 all-gather.11
  113.2 47.6 all-gather.13
  162.9 47.5 all-gather.15
where the time goes:
time: 333 us; the launch traced here: 332 us
  waiting for transfers between devices  172 us (52%)
  matrix products  67.7 us (20%)
  blocking collectives  44.6 us (13%)
  other arithmetic  16.9 us (5%)
  between operations  14.3 us (4%)
  local copies, waits for them, and re-layouts  10 us (3%)
  starting transfers between devices  6.16 us (2%)
    all_gather x1, waiting for transfers between devices, shards(): lax.all_gather(w_key[0], 'dp', axis=0, tiled=True)  47.3 us
    all_gather x1, waiting for transfers between devices, shards(): lax.all_gather(w_out[0], 'dp', axis=1, tiled=True)  47.2 us
    all_gather x1, waiting for transfers between devices, shards(): lax.all_gather(w_value[0], 'dp', axis=0, tiled=True)  47.2 us
    all_gather x1, blocking collectives, shards(): piece = lax.all_gather(blocks, 'dp', axis=0, tiled=True)  31.4 us
    all_gather x1, waiting for transfers between devices, shards(): lax.all_gather(w_query[0], 'dp', axis=0, tiled=True)  27.2 us
    dot_general x5, matrix products, section_forward(): jnp.dot(mixed, w_out, preferred_element_type=jnp.float32)  15.4 us
    dot_general x7, matrix products, section_forward(): jnp.dot(normed, w_value, preferred_element_type=jnp.float32)  14.6 us
    all_gather x1, blocking collectives, shards(): all_owner = lax.all_gather(owners[:, 0], 'dp', axis=0, tiled=True)  13.2 us
  transfers between devices with their start and end apart: 8, of which 6 were waited for; matrix products, arithmetic and copies ran while one was open for 10% of the time, Pallas kernels for 0%

commit v1 on v0

--- a/solution.py
+++ b/solution.py
@@ -6,6 +6,23 @@
 CAP = 4
 EPSILON = 1e-05
 MASKED = -1e30
+
+
+def laid_out(blocks, dim):
+    dims = list(blocks.shape[1:])
+    dims[dim] *= blocks.shape[0]
+    return jnp.moveaxis(blocks, 0, dim).reshape(dims)
+
+
+def collect(x, axis, dim):
+    count = lax.axis_size(axis)
+    ahead = [(i, (i + 1) % count) for i in range(count)]
+    blocks = [x]
+    while len(blocks) < count:
+        blocks.append(lax.ppermute(blocks[-1], axis, ahead))
+    index = lax.axis_index(axis)
+    blocks = jnp.stack(blocks)[(index - jnp.arange(count)) % count]
+    return laid_out(blocks, dim)
 
 
 def passed_along(array, axis, by):
@@ -86,7 +103,7 @@
     model_width = boundary.shape[3]
     proj_rank = proj_wide.shape[0]
     query_w, key_w, value_w, out_w = (
-        lax.all_gather(w_query[0], "dp", axis=0, tiled=True),
+        collect(w_query[0], "dp", 0),
         lax.all_gather(w_key[0], "dp", axis=0, tiled=True),
         lax.all_gather(w_value[0], "dp", axis=0, tiled=True),
         lax.all_gather(w_out[0], "dp", axis=1, tiled=True),

time: 333 us -> 309 us (0.928)
  waiting for transfers between devices: 172 us -> 119 us
  local copies, waits for them, and re-layouts: 10 us -> 20.9 us
  starting transfers between devices: 6.16 us -> 16.7 us
  other arithmetic: 16.9 us -> 22.1 us
  matrix products: 67.7 us -> 72.1 us
    ppermute x0 -> x7, waiting for transfers between devices: none -> 50.8 us  [collect(): blocks.append(lax.ppermute(blocks[-1], axis, ahead))]
    all_gather x1, waiting for transfers between devices: 47.3 us -> 0.01 us  [shards(): lax.all_gather(w_key[0], 'dp', axis=0, tiled=True)]
    all_gather x1, waiting for transfers between devices: 47.2 us -> 17.3 us  [shards(): lax.all_gather(w_value[0], 'dp', axis=0, tiled=True)]
    all_gather x1 -> x0, waiting for transfers between devices: 27.2 us -> none  [shards(): lax.all_gather(w_query[0], 'dp', axis=0, tiled=True)]
    ppermute x0 -> x7, starting transfers between devices: none -> 10.6 us  [collect(): blocks.append(lax.ppermute(blocks[-1], axis, ahead))]
    unnamed x33 -> x50, local copies, waits for them, and re-layouts: 5.87 us -> 12.2 us
    gather x0 -> x1, local copies, waits for them, and re-layouts: none -> 3.75 us  [collect(): blocks = jnp.stack(blocks)[(index - jnp.arange(count)) % count]]
    convert_element_type x2, other arithmetic: 3.39 us -> 7.01 us  [section_forward(): widened = hidden.astype(jnp.float32)]
  transfers between devices with their start and end apart: 8 -> 14, of which waited for: 6 -> 11; matrix products, arithmetic and copies ran while one was open for 10% -> 15% of each run, Pallas kernels for 0% -> 0%
where the time goes in v1:
time: 309 us; the launch traced here: 308 us
  waiting for transfers between devices  119 us (39%)
  matrix products  72.1 us (23%)
  blocking collectives  43.1 us (14%)
  other arithmetic  22.1 us (7%)
  local copies, waits for them, and re-layouts  20.9 us (7%)
  starting transfers between devices  16.7 us (5%)
  between operations  14.3 us (5%)
    ppermute x7, waiting for transfers between devices, collect(): blocks.append(lax.ppermute(blocks[-1], axis, ahead))  50.8 us
    all_gather x1, waiting for transfers between devices, shards(): lax.all_gather(w_out[0], 'dp', axis=1, tiled=True)  47.4 us
    all_gather x1, blocking collectives, shards(): piece = lax.all_gather(blocks, 'dp', axis=0, tiled=True)  31.4 us
    all_gather x1, waiting for transfers between devices, shards(): lax.all_gather(w_value[0], 'dp', axis=0, tiled=True)  17.3 us
    dot_general x5, matrix products, section_forward(): jnp.dot(mixed, w_out, preferred_element_type=jnp.float32)  15.4 us
    dot_general x7, matrix products, section_forward(): jnp.dot(normed, w_value, preferred_element_type=jnp.float32)  15.3 us
    unnamed x50, local copies, waits for them, and re-layouts  12.2 us
    dot_general x4, matrix products, section_forward(): jnp.dot(normed, w_query, preferred_element_type=jnp.float32)  12.1 us
  transfers between devices with their start and end apart: 14, of which 11 were waited for; matrix products, arithmetic and copies ran while one was open for 15% of the time, Pallas kernels for 0%

profile of v1, /device:TPU:0, one launch (start us, length us, event | category | flops | bytes accessed | tf_op | source)
XLA Modules:
  0.0 308.3 jit_solution(9465124294409455852)
XLA Ops:
  8.1 3.0 collective-permute-start
  21.4 11.7 %all-reduce = s32[16]{0:T(128)S(1)} all-reduce(s32[16]{0:T(128)S(1)} %bitcast_dynamic-update-slice_fusion.10), channel_id=2, replica_groups=mesh['groups'=2,'dp'=8,'section'=2] {'dp'}, use_global_device_ids=true, to_apply=%add | all-reduce | flops 16 | bytes 128 | tf_op jit(solution)/shard_map/all_gather | solution.py:111
  34.1 3.7 %collective-permute-done.1 = bf16[1024,128]{1,0:T(8,128)(2,1)} collective-permute-done((bf16[1024,128]{1,0:T(8,128)(2,1)}, bf16[1024,128]{1,0:T(8,128)(2,1)}, u32[]{:S(2)}, u32[]{:S(2)}) %collective-permute-start.1) | collective-permute-done | bytes 262176 | tf_op jit(solution)/shard_map/ppermute | solution.py:22
  37.8 3.7 %collective-permute-start.2 = (bf16[1024,128]{1,0:T(8,128)(2,1)}, bf16[1024,128]{1,0:T(8,128)(2,1)S(1)}, u32[]{:S(2)}, u32[]{:S(2)}) collective-permute-start(bf16[1024,128]{1,0:T(8,128)(2,1)} %collective-permute-done.1), channel_id=1, source_target_pairs={{0,2},{2,4},{4,6},{6,8},{8,10},{10,12},{12,14},{14,0},{1,3},{3,5},... | collective-permute-start | bytes 786440 | tf_op jit(solution)/shard_map/ppermute | solution.py:22
  44.7 7.6 %collective-permute-done.2 = bf16[1024,128]{1,0:T(8,128)(2,1)S(1)} collective-permute-done((bf16[1024,128]{1,0:T(8,128)(2,1)}, bf16[1024,128]{1,0:T(8,128)(2,1)S(1)}, u32[]{:S(2)}, u32[]{:S(2)}) %collective-permute-start.2) | collective-permute-done | bytes 262176 | tf_op jit(solution)/shard_map/ppermute | solution.py:22
  56.3 9.7 %collective-permute-done.3 = bf16[1024,128]{1,0:T(8,128)(2,1)S(1)} collective-permute-done((bf16[1024,128]{1,0:T(8,128)(2,1)S(1)}, bf16[1024,128]{1,0:T(8,128)(2,1)S(1)}, u32[]{:S(2)}, u32[]{:S(2)}) %collective-permute-start.3) | collective-permute-done | bytes 262176 | tf_op jit(solution)/shard_map/ppermute | solution.py:22
  70.5 6.4 %collective-permute-done.4 = bf16[1024,128]{1,0:T(8,128)(2,1)S(1)} collective-permute-done((bf16[1024,128]{1,0:T(8,128)(2,1)S(1)}, bf16[1024,128]{1,0:T(8,128)(2,1)S(1)}, u32[]{:S(2)}, u32[]{:S(2)}) %collective-permute-start.4) | collective-permute-done | bytes 262176 | tf_op jit(solution)/shard_map/ppermute | solution.py:22
  78.7 8.2 %collective-permute-done.5 = bf16[1024,128]{1,0:T(8,128)(2,1)S(1)} collective-permute-done((bf16[1024,128]{1,0:T(8,128)(2,1)S(1)}, bf16[1024,128]{1,0:T(8,128)(2,1)S(1)}, u32[]{:S(2)}, u32[]{:S(2)}) %collective-permute-start.5) | collective-permute-done | bytes 262176 | tf_op jit(solution)/shard_map/ppermute | solution.py:22
  88.4 13.3 %collective-permute-done.6 = bf16[1024,128]{1,0:T(8,128)(2,1)S(1)} collective-permute-done((bf16[1024,128]{1,0:T(8,128)(2,1)S(1)}, bf16[1024,128]{1,0:T(8,128)(2,1)S(1)}, u32[]{:S(2)}, u32[]{:S(2)}) %collective-permute-start.6) | collective-permute-done | bytes 262176 | tf_op jit(solution)/shard_map/ppermute | solution.py:22
  102.4 3.7 %gather_fusion = bf16[8,1024,128]{2,1,0:T(8,128)(2,1)} fusion(bf16[8,1024,128]{2,1,0:T(8,128)(2,1)} %bitcast_dynamic-update-slice_fusion.3, s32[1024]{0:T(1024)S(1)} %pad_clamp_fusion), kind=kCustom, calls=%fused_computation | custom fusion | bytes 4194336 | tf_op jit(solution)/shard_map/gather | solution.py:24
  106.1 2.5 fusion.92
  108.6 2.6 fusion.298
  111.2 17.3 %all-gather.10.cloned.1.call-done = bf16[1,8192,128]{2,1,0:T(8,128)(2,1)} async-done(((bf16[1,1024,128]{2,1,0:T(8,128)(2,1)}), bf16[1,8192,128]{2,1,0:T(8,128)(2,1)}) %all-gather.10.cloned.1.call-update) | async-done | bytes 2097168 | tf_op jit(solution)/shard_map/all_gather | solution.py:108
  128.6 2.5 fusion.107
  131.0 47.4 %all-gather.12.cloned.1.call-done = bf16[1,128,8192]{2,1,0:T(8,128)(2,1)} async-done(((bf16[1,128,1024]{2,1,0:T(8,128)(2,1)}), bf16[1,128,8192]{2,1,0:T(8,128)(2,1)}) %all-gather.12.cloned.1.call-update) | async-done | bytes 2097168 | tf_op jit(solution)/shard_map/all_gather | solution.py:109
  178.4 3.6 %fusion = bf16[64,8192]{1,0:T(8,128)(2,1)} fusion(bf16[1,128,8192]{2,1,0:T(8,128)(2,1)} %all-gather.12.cloned.1.call-done, bf16[64,128]{1,0:T(8,128)(2,1)S(1)} %fusion.107, f32[64,64]{0,1:T(8,128)S(1)} %get-tuple-element.27, f32[64]{0:T(128)S(1)} %fusion.178, f32[64]{0:T(128)S(1)} %get-tuple-element.26, bf16[1,2,64,8192]{3,2,1,0:T(8,128)(2,1)} %param.10, ...), kind=kOutput, calls=%fused_computation.3 | convolution fusion | flops 137383936 | bytes 4227589 | tf_op jit(solution)/shard_map/dot_general | solution.py:64
  184.6 2.5 fusion.122
  189.5 2.6 fusion.301
  192.1 2.4 fusion.110
  194.5 3.4 %fusion.1 = bf16[64,8192]{1,0:T(8,128)(2,1)} fusion(bf16[64,8192]{1,0:T(8,128)(2,1)} %copy-done.6, bf16[1,128,8192]{2,1,0:T(8,128)(2,1)} %all-gather.12.cloned.1.call-done, bf16[64,128]{1,0:T(8,128)(2,1)S(1)} %fusion.110, f32[64,64]{0,1:T(8,128)S(1)} %get-tuple-element.29, f32[64]{0:T(128)S(1)} %fusion.179, f32[64]{0:T(128)S(1)} %get-tuple-element.28), kind=kOutput, calls=%fused_computation.4 | convolution fusion | flops 136859648 | bytes 4227584 | tf_op jit(solution)/shard_map/dot_general | solution.py:64
  209.4 3.6 %convolution_convert_fusion.4 = bf16[64,8192]{1,0:T(8,128)(2,1)} fusion(bf16[1,8192,128]{2,1,0:T(8,128)(2,1)} %all-gather.8.cloned.1.call-done, bf16[64,128]{1,0:T(8,128)(2,1)S(1)} %convolution_convert_fusion.33, f32[64,64]{0,1:T(8,128)S(1)} %get-tuple-element.14, pred[64,64]{0,1:T(32,128)(4,1)S(1)} %get-tuple-element.16, f32[64]{0:T(128)S(1)} %negate_divide_fusion.1, ...), kind=kOutput, calls=%fused_computation.9 | convolution fusion | flops 135823360 | bytes 3182912 | tf_op jit(solution)/shard_map/transpose(jvp())/dot_general | solution.py:49
  212.9 3.7 %fusion.2 = bf16[64,8192]{1,0:T(8,128)(2,1)} fusion(bf16[64,8192]{1,0:T(8,128)(2,1)} %convolution_convert_fusion.4, bf16[64,128]{1,0:T(8,128)(2,1)S(1)} %convolution_convert_fusion.32, bf16[1,8192,128]{2,1,0:T(8,128)(2,1)} %all-gather.10.cloned.1.call-done), kind=kOutput, calls=%fused_computation.11 | convolution fusion | flops 135266304 | bytes 4210688 | tf_op jit(solution)/shard_map/transpose(jvp())/dot_general | solution.py:51
  216.6 4.6 %fusion.25 = (f32[64]{0:T(128)S(1)}, f32[64]{0:T(128)S(1)}, f32[64,8192]{1,0:T(8,128)}) fusion(bf16[2,64,8192]{2,1,0:T(8,128)(2,1)S(1)} %bitcast_dynamic-update-slice_fusion, s32[]{:T(128)S(6)} %min.19, s32[]{:T(128)S(6)} %min.23, f32[8192]{0:T(1024)S(1)} %bitcast.332, bf16[64,8192]{1,0:T(8,128)(2,1)} %fusion.2, bf16[8192,128]{1,0:T(8,128)(2,1)} %bitcast.317, ...), kind=kOutput, calls=%fused_computation.47 | convolution fusion | flops 141590400 | bytes 7410504 | tf_op jit(solution)/shard_map/transpose(jvp())/dot_general | solution.py:48
  223.6 3.4 %fusion.47 = bf16[64,8192]{1,0:T(8,128)(2,1)} fusion(f32[64,8192]{1,0:T(8,128)} %get-tuple-element.33, f32[64]{0:T(128)S(1)} %multiply_multiply_fusion.1, f32[64]{0:T(128)S(1)} %fusion.252, bf16[2,64,8192]{2,1,0:T(8,128)(2,1)S(1)} %bitcast_dynamic-update-slice_fusion, s32[]{:T(128)S(6)} %min.19, bf16[1,2,64,8192]{3,2,1,0:T(8,128)(2,1)S(1)} %copy-done.4, ...), kind=kLoop, calls=%fused_computation.69 | loop fusion | flops 5242880 | bytes 5243461 | tf_op jit(solution)/shard_map/transpose(jvp())/convert_element_type | solution.py:45
  232.0 2.7 fusion.150
  236.5 2.8 fusion.125
  239.8 3.6 %convolution_convert_fusion.1 = bf16[64,8192]{1,0:T(8,128)(2,1)} fusion(bf16[1,8192,128]{2,1,0:T(8,128)(2,1)} %all-gather.8.cloned.1.call-done, bf16[64,128]{1,0:T(8,128)(2,1)S(1)} %convolution_convert_fusion.26, f32[64,64]{0,1:T(8,128)S(1)} %get-tuple-element.10, pred[64,64]{0,1:T(32,128)(4,1)S(1)} %get-tuple-element.12, f32[64]{0:T(128)S(1)} %negate_divide_fusion, ...), kind=kOutput, calls=%fused_computation.6 | convolution fusion | flops 135823360 | bytes 3182912 | tf_op jit(solution)/shard_map/transpose(jvp())/dot_general | solution.py:49
  243.3 3.7 %fusion.6 = bf16[64,8192]{1,0:T(8,128)(2,1)} fusion(bf16[64,8192]{1,0:T(8,128)(2,1)} %convolution_convert_fusion.1, bf16[64,128]{1,0:T(8,128)(2,1)S(1)} %convolution_convert_fusion.22, bf16[1,8192,128]{2,1,0:T(8,128)(2,1)} %all-gather.10.cloned.1.call-done), kind=kOutput, calls=%fused_computation.15 | convolution fusion | flops 135266304 | bytes 4210688 | tf_op jit(solution)/shard_map/transpose(jvp())/dot_general | solution.py:51
  247.0 4.6 %fusion.31 = (f32[64]{0:T(128)S(1)}, f32[64]{0:T(128)S(1)}, f32[64,8192]{1,0:T(8,128)}) fusion(bf16[2,64,8192]{2,1,0:T(8,128)(2,1)S(1)} %bitcast_dynamic-update-slice_fusion, s32[]{:T(128)S(6)} %min.23, s32[]{:T(128)S(6)} %min.24, f32[8192]{0:T(1024)S(1)} %bitcast.336, bf16[64,8192]{1,0:T(8,128)(2,1)} %fusion.6, bf16[8192,128]{1,0:T(8,128)(2,1)} %bitcast.319, ...), kind=kOutput, calls=%fused_computation.53 | convolution fusion | flops 141590400 | bytes 7410504 | tf_op jit(solution)/shard_map/transpose(jvp())/dot_general | solution.py:48
  251.7 3.6 %fusion.48 = bf16[64,8192]{1,0:T(8,128)(2,1)} fusion(f32[64,8192]{1,0:T(8,128)} %get-tuple-element.37, bf16[64,8192]{1,0:T(8,128)(2,1)} %fusion.150, f32[64]{0:T(128)S(1)} %multiply_multiply_fusion, f32[64]{0:T(128)S(1)} %fusion.253, bf16[2,64,8192]{2,1,0:T(8,128)(2,1)S(1)} %bitcast_dynamic-update-slice_fusion, s32[]{:T(128)S(6)} %min.23), kind=kLoop, calls=%fused_computation.70 | loop fusion | flops 4194304 | bytes 5243396 | tf_op jit(solution)/shard_map/transpose(jvp())/convert_element_type | solution.py:45
  262.7 3.1 %fusion.128 = bf16[64,128]{1,0:T(8,128)(2,1)S(1)} fusion(bf16[1,128,8192]{2,1,0:T(8,128)(2,1)} %all-gather.12.cloned.1.call-done, bf16[64,8192]{1,0:T(8,128)(2,1)} %collective-permute-done.10, bf16[1,2,64,8192]{3,2,1,0:T(8,128)(2,1)} %param.10, s32[]{:T(128)S(6)} %min.24, pred[64]{0:T(512)(128)(4,1)S(1)} %copy-done.17, pred[]{:T(512)S(6)} %eq.66), kind=kOutput, calls=%fused_computation.137 | convolution fusion | flops 135274496 | bytes 4210757 | tf_op jit(solution)/shard_map/transpose(jvp())/dot_general | solution.py:64
  268.9 31.4 %all_gather.19 = bf16[16,2,64,64]{3,2,1,0:T(8,128)(2,1)S(1)} all-gather(bf16[2,2,64,64]{3,2,1,0:T(8,128)(2,1)S(1)} %fusion.172), channel_id=1, replica_groups=mesh['groups'=2,'dp'=8,'section'=2] {'dp'}, dimensions={0}, use_global_device_ids=true | all-gather | bytes 294912 | tf_op jit(solution)/shard_map/all_gather | solution.py:175
  (147 shorter events, 65.5 us)
Async XLA Ops:
  6.5 200.1 %copy-start = (bf16[64,8192]{1,0:T(8,128)(2,1)S(1)}, bf16[64,8192]{1,0:T(8,128)(2,1)}, u32[]{:S(2)}) copy-start(bf16[64,8192]{1,0:T(8,128)(2,1)} %param.16) | copy-start | bytes 3145732
  6.5 99.6 %all-gather.8.cloned.1.call-start = ((), (), s32[]{:S(2)}) async-start(), calls=%async_computation | async-start | bytes 2359296 | tf_op jit(solution)/shard_map/all_gather | solution.py:107
  7.3 121.3 %all-gather.10.cloned.1.call-start = ((), (), s32[]{:S(2)}) async-start(), calls=%async_computation.1 | async-start | bytes 2359296 | tf_op jit(solution)/shard_map/all_gather | solution.py:108
  8.0 170.4 %all-gather.12.cloned.1.call-start = ((), (), s32[]{:S(2)}) async-start(), calls=%async_computation.2 | async-start | bytes 2359296 | tf_op jit(solution)/shard_map/all_gather | solution.py:109
  8.1 12.7 %collective-permute-start = (bf16[1024,128]{1,0:T(8,128)(2,1)}, bf16[1024,128]{1,0:T(8,128)(2,1)}, u32[]{:S(2)}, u32[]{:S(2)}) collective-permute-start(bf16[1024,128]{1,0:T(8,128)(2,1)} %bitcast.342), channel_id=1, source_target_pairs={{0,2},{2,4},{4,6},{6,8},{8,10},{10,12},{12,14},{14,0},{1,3},{3,5},... | collective-permute-start | bytes 786440 | tf_op jit(solution)/shard_map/ppermute | solution.py:22
  13.8 2.9 copy-start.1
  16.6 16.8 %copy-start.13 = (bf16[1,1024,128]{2,1,0:T(8,128)(2,1)S(1)}, bf16[1,1024,128]{2,1,0:T(8,128)(2,1)}, u32[]{:S(2)}) copy-start(bf16[1,1024,128]{2,1,0:T(8,128)(2,1)} %param.11) | copy-start | bytes 786436
  20.7 17.1 %collective-permute-start.1 = (bf16[1024,128]{1,0:T(8,128)(2,1)}, bf16[1024,128]{1,0:T(8,128)(2,1)}, u32[]{:S(2)}, u32[]{:S(2)}) collective-permute-start(bf16[1024,128]{1,0:T(8,128)(2,1)} %collective-permute-done), channel_id=1, source_target_pairs={{0,2},{2,4},{4,6},{6,8},{8,10},{10,12},{12,14},{14,0},{1,3},{3,5},... | collective-permute-start | bytes 786440 | tf_op jit(solution)/shard_map/ppermute | solution.py:22
  37.8 14.5 %collective-permute-start.2 = (bf16[1024,128]{1,0:T(8,128)(2,1)}, bf16[1024,128]{1,0:T(8,128)(2,1)S(1)}, u32[]{:S(2)}, u32[]{:S(2)}) collective-permute-start(bf16[1024,128]{1,0:T(8,128)(2,1)} %collective-permute-done.1), channel_id=1, source_target_pairs={{0,2},{2,4},{4,6},{6,8},{8,10},{10,12},{12,14},{14,0},{1,3},{3,5},... | collective-permute-start | bytes 786440 | tf_op jit(solution)/shard_map/ppermute | solution.py:22
  52.3 13.7 %collective-permute-start.3 = (bf16[1024,128]{1,0:T(8,128)(2,1)S(1)}, bf16[1024,128]{1,0:T(8,128)(2,1)S(1)}, u32[]{:S(2)}, u32[]{:S(2)}) collective-permute-start(bf16[1024,128]{1,0:T(8,128)(2,1)S(1)} %collective-permute-done.2), channel_id=1, source_target_pairs={{0,2},{2,4},{4,6},{6,8},{8,10},{10,12},{12,14},{14,0},{1,3},{3,5},... | collective-permute-start | bytes 786440 | tf_op jit(solution)/shard_map/ppermute | solution.py:22
  66.0 11.0 %collective-permute-start.4 = (bf16[1024,128]{1,0:T(8,128)(2,1)S(1)}, bf16[1024,128]{1,0:T(8,128)(2,1)S(1)}, u32[]{:S(2)}, u32[]{:S(2)}) collective-permute-start(bf16[1024,128]{1,0:T(8,128)(2,1)S(1)} %collective-permute-done.3), channel_id=1, source_target_pairs={{0,2},{2,4},{4,6},{6,8},{8,10},{10,12},{12,14},{14,0},{1,3},{3,5},... | collective-permute-start | bytes 786440 | tf_op jit(solution)/shard_map/ppermute | solution.py:22
  77.0 10.0 %collective-permute-start.5 = (bf16[1024,128]{1,0:T(8,128)(2,1)S(1)}, bf16[1024,128]{1,0:T(8,128)(2,1)S(1)}, u32[]{:S(2)}, u32[]{:S(2)}) collective-permute-start(bf16[1024,128]{1,0:T(8,128)(2,1)S(1)} %collective-permute-done.4), channel_id=1, source_target_pairs={{0,2},{2,4},{4,6},{6,8},{8,10},{10,12},{12,14},{14,0},{1,3},{3,5},... | collective-permute-start | bytes 786440 | tf_op jit(solution)/shard_map/ppermute | solution.py:22
  86.9 14.7 %collective-permute-start.6 = (bf16[1024,128]{1,0:T(8,128)(2,1)S(1)}, bf16[1024,128]{1,0:T(8,128)(2,1)S(1)}, u32[]{:S(2)}, u32[]{:S(2)}) collective-permute-start(bf16[1024,128]{1,0:T(8,128)(2,1)S(1)} %collective-permute-done.5), channel_id=1, source_target_pairs={{0,2},{2,4},{4,6},{6,8},{8,10},{10,12},{12,14},{14,0},{1,3},{3,5},... | collective-permute-start | bytes 786440 | tf_op jit(solution)/shard_map/ppermute | solution.py:22
  106.1 2.5 copy-start.19
  182.0 2.6 copy-start.2
  182.0 5.1 %collective-permute-start.7 = (bf16[64,8192]{1,0:T(8,128)(2,1)}, bf16[64,8192]{1,0:T(8,128)(2,1)S(1)}, u32[]{:S(2)}, u32[]{:S(2)}) collective-permute-start(bf16[64,8192]{1,0:T(8,128)(2,1)} %fusion), channel_id=1, source_target_pairs={{0,1},{2,3},{4,5},{6,7},{8,9},{10,11},{12,13},{14,15},{16,17},{18,... | collective-permute-start | bytes 3145736 | tf_op jit(solution)/shard_map/ppermute | solution.py:31
  187.1 1.9 copy-start.9
  187.6 1.0 copy-start.6
  187.6 1.9 copy-start.18
  198.0 3.9 %copy-start.3 = (bf16[1,2,64,8192]{3,2,1,0:T(8,128)(2,1)S(1)}, bf16[1,2,64,8192]{3,2,1,0:T(8,128)(2,1)}, u32[]{:S(2)}) copy-start(bf16[1,2,64,8192]{3,2,1,0:T(8,128)(2,1)} %param.10) | copy-start | bytes 6291460
  198.0 3.9 %collective-permute-start.8 = (bf16[64,8192]{1,0:T(8,128)(2,1)}, bf16[64,8192]{1,0:T(8,128)(2,1)S(1)}, u32[]{:S(2)}, u32[]{:S(2)}) collective-permute-start(bf16[64,8192]{1,0:T(8,128)(2,1)} %fusion.1), channel_id=1, source_target_pairs={{0,1},{2,3},{4,5},{6,7},{8,9},{10,11},{12,13},{14,15},{16,17},{18,... | collective-permute-start | bytes 3145736 | tf_op jit(solution)/shard_map/ppermute | solution.py:31
  201.6 1.6 copy-start.5
  202.4 1.7 copy-start.10
  204.1 1.6 copy-start.7
  204.6 1.6 copy-start.14
  221.3 2.3 copy-start.4
  223.6 4.9 %copy-start.11 = (bf16[1,8192,128]{2,1,0:T(8,128)(2,1)S(1)}, bf16[1,8192,128]{2,1,0:T(8,128)(2,1)}, u32[]{:S(2)}) copy-start(bf16[1,8192,128]{2,1,0:T(8,128)(2,1)} %all-gather.8.cloned.1.call-done) | copy-start | bytes 6291460
  227.0 2.2 copy-start.8
  227.0 5.0 %collective-permute-start.9 = (bf16[64,8192]{1,0:T(8,128)(2,1)}, bf16[64,8192]{1,0:T(8,128)(2,1)}, u32[]{:S(2)}, u32[]{:S(2)}) collective-permute-start(bf16[64,8192]{1,0:T(8,128)(2,1)} %fusion.47), channel_id=1, source_target_pairs={{1,0},{3,2},{5,4},{7,6},{9,8},{11,10},{13,12},{15,14},{17,16},{19,... | collective-permute-start | bytes 3145736 | tf_op jit(solution)/shard_map/ppermute | solution.py:31
  251.7 5.1 %copy-start.12 = (bf16[1,8192,128]{2,1,0:T(8,128)(2,1)S(1)}, bf16[1,8192,128]{2,1,0:T(8,128)(2,1)}, u32[]{:S(2)}) copy-start(bf16[1,8192,128]{2,1,0:T(8,128)(2,1)} %all-gather.8.cloned.1.call-done) | copy-start | bytes 6291460
  255.3 7.4 %collective-permute-start.10 = (bf16[64,8192]{1,0:T(8,128)(2,1)}, bf16[64,8192]{1,0:T(8,128)(2,1)}, u32[]{:S(2)}, u32[]{:S(2)}) collective-permute-start(bf16[64,8192]{1,0:T(8,128)(2,1)} %fusion.48), channel_id=1, source_target_pairs={{1,0},{3,2},{5,4},{7,6},{9,8},{11,10},{13,12},{15,14},{17,16},{19,... | collective-permute-start | bytes 3145736 | tf_op jit(solution)/shard_map/ppermute | solution.py:31
  266.7 34.0 %copy-start.15 = (pred[16]{0:T(512)(128)(4,1)S(1)}, pred[16]{0:T(512)(128)(4,1)}, u32[]{:S(2)}) copy-start(pred[16]{0:T(512)(128)(4,1)} %broadcast_compare_fusion.2) | copy-start | bytes 52
  (2 other events, 1.6 us)
Sparse Core Ops, SparseCore 0:
  9.5 63.0 all-gather.7
  74.7 53.7 all-gather.9
  130.7 47.5 all-gather.11
